TPU v7x, 256 devices: a whole 4x4x8 slice. The times are simulated.
256 devices in a mesh: outer: 16 (over z_hi, x, core), inner: 16 (over z_lo, y).
Axes of the slice: x: 4, y: 4, z: 8 (z_hi: 2, z_lo: 4; z = z_hi * 4 + z_lo), core: 2. Of those that a mesh axis runs over, the one named last changes fastest.
Arguments:
- tokens: bfloat16 [65536, 2048], P(('outer', 'inner')), may hold values from -6 to 6
- w_qkv: bfloat16 [2048, 3072], P('inner'), may hold values from -2.8 to 2.8
- w_out: bfloat16 [1024, 2048], P(None, 'inner'), may hold values from -1.5 to 1.5
- neighbours: int32 [256, 5], P(('outer', 'inner')), may hold values from -1 to 255, as said below
- counts: int32 [256], replicated, may hold values from 1 to 256, as said below
Outputs:
- attended: bfloat16 [65536, 2048], P(('outer', 'inner'))
Inputs may be any that keep to these rules, and one draw needn't show every extreme that they name: `neighbours`: slot 0 of row b is b itself; slots 1 and 2 are the blocks b - 16 and b + 16 (the same inner index in the previous and next slab of outer), slots 3 and 4 the blocks b - 1 and b + 1 of the same slab; a slot holds -1 where its block lies outside the grid of blocks, and may hold -1 otherwise. `counts`: some block is full.
All inputs are finite; a program needn't handle non-finite values.
Results may differ from a plain program's by a relative error of at most 0.0093.
Values may be sent and summed in bfloat16 or wider, within the bound.
A program may use at most 64 MiB of HBM per device.

v0:
```python
import jax
import jax.numpy as jnp
from jax import lax
from jax.sharding import PartitionSpec as P

HD = 128


def padded(block, sides, width):
    for axis, dim in sides:
        count = lax.axis_size(axis)
        forward = [(i, i + 1) for i in range(count - 1)]
        backward = [(target, source) for source, target in forward]
        low = lax.ppermute(
            lax.slice_in_dim(block, block.shape[dim] - width, None, axis=dim), axis, forward
        )
        high = lax.ppermute(lax.slice_in_dim(block, 0, width, axis=dim), axis, backward)
        block = jnp.concatenate([low, block, high], axis=dim)
    return block


def normalize(values_in):
    values = values_in.astype(jnp.float32)
    center = values - jnp.mean(values, axis=-1, keepdims=True)
    spread = jnp.mean(center * center, axis=-1, keepdims=True)
    return (center * lax.rsqrt(spread + 1e-05)).astype(jnp.bfloat16)


def per_device(tokens, w_qkv, w_out, neighbours, counts):
    normed = normalize(tokens)
    rows_here = normed.shape[0]
    heads_all = w_out.shape[0]
    head_size = HD
    projected = jnp.dot(
        normed,
        lax.all_gather(w_qkv, "inner", axis=0, tiled=True),
        preferred_element_type=jnp.float32,
    ).astype(jnp.bfloat16)
    queries = projected[:, :heads_all]
    keys_values = projected[:, heads_all:]
    slab_halo = padded(keys_values[None], (("outer", 0),), 1)
    row_halo = padded(keys_values[None], (("inner", 0),), 1)
    candidates = (keys_values, slab_halo[0], slab_halo[2], row_halo[0], row_halo[2])
    listed = neighbours[0]
    clipped = jnp.maximum(listed, 0)
    block_ids = jnp.arange(counts.shape[0], dtype=jnp.int32)
    lengths = jnp.sum(jnp.where(clipped[:, None] == block_ids[None, :], counts[None, :], 0), axis=1)
    positions = jnp.arange(rows_here, dtype=jnp.int32)
    usable = (listed[:, None] >= 0) & (positions[None, :] < lengths[:, None])
    allowed = usable.reshape(-1)
    score_scale = float(head_size) ** (-0.5)
    outputs = []
    for head_index in range(heads_all // head_size):
        offset_q = head_index * head_size
        offset_v = heads_all + offset_q
        query_head = queries[:, offset_q : offset_q + head_size]
        scores = (
            jnp.concatenate(
                [
                    jnp.einsum(
                        "qd,kd->qk",
                        query_head,
                        source_kv[:, offset_q : offset_q + head_size],
                        preferred_element_type=jnp.float32,
                    )
                    for source_kv in candidates
                ],
                axis=1,
            )
            * score_scale
        )
        masked = jnp.where(allowed[None, :], scores, -jnp.inf)
        largest = jnp.max(masked, axis=1, keepdims=True)
        weights = jnp.exp(masked - largest)
        totals = jnp.sum(weights, axis=1, keepdims=True)
        rounded = weights.astype(jnp.bfloat16)
        context = jnp.zeros((rows_here, head_size), jnp.float32)
        for slot_no in range(len(candidates)):
            context = context + jnp.dot(
                rounded[:, slot_no * rows_here : (slot_no + 1) * rows_here],
                candidates[slot_no][:, offset_v : offset_v + head_size],
                preferred_element_type=jnp.float32,
            )
        outputs.append((context / totals).astype(jnp.bfloat16))
    context_all = jnp.concatenate(outputs, axis=1)
    return jnp.dot(
        context_all,
        lax.all_gather(w_out, "inner", axis=1, tiled=True),
        preferred_element_type=jnp.float32,
    ).astype(jnp.bfloat16)


def solution(mesh):
    placed = (
        P(("outer", "inner"), None),
        P("inner", None),
        P(None, "inner"),
        P(("outer", "inner"), None),
        P(),
    )
    return jax.shard_map(
        per_device,
        mesh=mesh,
        in_specs=placed,
        out_specs=P(("outer", "inner"), None),
        check_vma=False,
    )
```

profile of v0, /device:TPU:152, one launch (start us, length us, event | category | flops | bytes accessed | tf_op | source)
XLA Modules:
  0.0 284.8 jit_solution(12477237379816694622)
XLA Ops:
  6.5 0.7 all-gather.3.cloned.1.call-update
  7.3 0.7 all-gather.5.cloned.1.call-update
  8.0 0.7 maximum_bitcast_fusion
  8.7 0.7 compare_bitcast_fusion
  9.3 0.2 convert_reduce_fusion
  9.6 0.4 fusion.2
  10.3 139.8 %all-gather.3.cloned.1.call-done = bf16[2048,3072]{1,0:T(8,128)(2,1)} async-done(((bf16[128,3072]{1,0:T(8,128)(2,1)}), bf16[2048,3072]{1,0:T(8,128)(2,1)}) %all-gather.3.cloned.1.call-update) | async-done | bytes 12582928 | tf_op jit(solution)/shard_map/all_gather | solution.py:36
  150.1 8.2 %convolution_convert_fusion = bf16[256,3072]{1,0:T(8,128)(2,1)S(1)} fusion(bf16[2048,3072]{1,0:T(8,128)(2,1)} %all-gather.3.cloned.1.call-done, bf16[256,2048]{1,0:T(8,128)(2,1)S(1)} %copy-done, f32[256]{0:T(256)S(1)} %add_rsqrt_fusion, f32[256]{0:T(256)S(1)} %broadcast_multiply_fusion), kind=kOutput, calls=%fused_computation | convolution fusion | flops 3224109056 | bytes 15206400 | tf_op jit(solution)/shard_map/dot_general | solution.py:34
  158.5 1.9 collective-permute-start
  160.4 9.7 %collective-permute-start.1 = (bf16[1,256,2048]{2,1,0:T(8,128)(2,1)S(1)}, bf16[1,256,2048]{2,1,0:T(8,128)(2,1)S(1)}, u32[]{:S(2)}, u32[]{:S(2)}) collective-permute-start(bf16[1,256,2048]{2,1,0:T(8,128)(2,1)S(1)} %slice_bitcast_fusion), channel_id=1, source_target_pairs={{16,0},{32,16},{48,32},{64,48},{80,64},{96,80},{112,96},{128,112},... | collective-permute-start | bytes 3145736 | tf_op jit(solution)/shard_map/ppermute | solution.py:17
  170.1 5.2 %collective-permute-start.2 = (bf16[1,256,2048]{2,1,0:T(8,128)(2,1)S(1)}, bf16[1,256,2048]{2,1,0:T(8,128)(2,1)S(1)}, u32[]{:S(2)}, u32[]{:S(2)}) collective-permute-start(bf16[1,256,2048]{2,1,0:T(8,128)(2,1)S(1)} %slice_bitcast_fusion), channel_id=1, source_target_pairs={{0,1},{1,2},{2,3},{3,4},{4,5},{5,6},{6,7},{7,8},{8,9},{9,10},{10,1... | collective-permute-start | bytes 3145736 | tf_op jit(solution)/shard_map/ppermute | solution.py:14
  175.3 2.1 collective-permute-start.3
  178.8 20.7 %collective-permute-done = bf16[1,256,2048]{2,1,0:T(8,128)(2,1)S(1)} collective-permute-done((bf16[1,256,2048]{2,1,0:T(8,128)(2,1)S(1)}, bf16[1,256,2048]{2,1,0:T(8,128)(2,1)S(1)}, u32[]{:S(2)}, u32[]{:S(2)}) %collective-permute-start) | collective-permute-done | bytes 1048608 | tf_op jit(solution)/shard_map/ppermute | solution.py:14
  199.7 0.2 convolution_dynamic-update-slice_fusion.38
  199.9 6.6 %collective-permute-done.1 = bf16[1,256,2048]{2,1,0:T(8,128)(2,1)S(1)} collective-permute-done((bf16[1,256,2048]{2,1,0:T(8,128)(2,1)S(1)}, bf16[1,256,2048]{2,1,0:T(8,128)(2,1)S(1)}, u32[]{:S(2)}, u32[]{:S(2)}) %collective-permute-start.1) | collective-permute-done | bytes 1048608 | tf_op jit(solution)/shard_map/ppermute | solution.py:17
  206.7 0.2 convolution_dynamic-update-slice_fusion.37
  206.9 21.2 %collective-permute-done.2 = bf16[1,256,2048]{2,1,0:T(8,128)(2,1)S(1)} collective-permute-done((bf16[1,256,2048]{2,1,0:T(8,128)(2,1)S(1)}, bf16[1,256,2048]{2,1,0:T(8,128)(2,1)S(1)}, u32[]{:S(2)}, u32[]{:S(2)}) %collective-permute-start.2) | collective-permute-done | bytes 1048608 | tf_op jit(solution)/shard_map/ppermute | solution.py:14
  228.4 26.1 %collective-permute-done.3 = bf16[1,256,2048]{2,1,0:T(8,128)(2,1)S(1)} collective-permute-done((bf16[1,256,2048]{2,1,0:T(8,128)(2,1)S(1)}, bf16[1,256,2048]{2,1,0:T(8,128)(2,1)S(1)}, u32[]{:S(2)}, u32[]{:S(2)}) %collective-permute-start.3) | collective-permute-done | bytes 1048608 | tf_op jit(solution)/shard_map/ppermute | solution.py:17
  255.3 0.2 convolution_dynamic-update-slice_fusion.31
  255.7 0.2 convolution_dynamic-update-slice_fusion.28
  259.6 0.4 fusion.11
  259.9 2.0 fusion.69
  261.9 0.2 fusion.127
  262.1 0.2 fusion.129
  262.4 0.2 fusion.133
  262.6 2.3 fusion.67
  264.9 0.2 fusion.119
  265.1 0.2 fusion.121
  265.3 0.2 fusion.125
  265.6 0.2 fusion.111
  265.8 0.2 fusion.113
  266.0 0.2 fusion.117
  266.2 0.2 fusion.103
  266.5 0.2 fusion.105
  266.7 0.2 fusion.109
  266.9 0.2 fusion.95
  267.2 0.2 fusion.97
  267.4 0.2 fusion.101
  267.6 0.2 fusion.87
  267.9 0.2 fusion.89
  268.1 0.2 fusion.93
  268.3 0.2 fusion.79
  268.5 0.2 fusion.81
  268.8 0.2 fusion.85
  269.0 0.2 fusion.71
  269.2 0.2 fusion.73
  269.5 0.2 fusion.77
  269.7 0.2 convolution_add_fusion.15
  269.9 0.2 convolution_add_fusion.13
  270.2 0.2 convolution_add_fusion.11
  270.4 0.2 convolution_add_fusion.9
  270.6 0.2 convolution_add_fusion.7
  270.9 0.2 convolution_add_fusion.5
  271.1 0.2 convolution_add_fusion.3
  271.3 0.2 convolution_add_fusion.1
  271.5 0.2 fusion.51
  271.8 0.2 fusion.49
  272.0 0.2 fusion.47
  272.3 0.2 fusion.45
  272.5 0.2 fusion.43
  272.8 0.2 fusion.41
  273.1 0.2 fusion.39
  273.3 0.2 fusion.37
  273.6 4.4 %convolution_convert_fusion.1 = bf16[256,2048]{1,0:T(8,128)(2,1)} fusion(bf16[256,1024]{1,0:T(8,128)(2,1)S(1)} %fusion.37, bf16[1024,2048]{1,0:T(8,128)(2,1)} %all-gather.5.cloned.1.call-done), kind=kOutput, calls=%fused_computation.3 | convolution fusion | flops 1074266112 | bytes 5767168 | tf_op jit(solution)/shard_map/dot_general | solution.py:86
  (49 shorter events, 7.1 us)
Async XLA Ops:
  6.5 2.8 copy-start
  6.5 143.5 %all-gather.3.cloned.1.call-start = ((), (), s32[]{:S(2)}) async-start(), calls=%async_computation | async-start | bytes 13369344 | tf_op jit(solution)/shard_map/all_gather | solution.py:36
  7.3 2.7 copy-start.1
  7.3 266.3 %all-gather.5.cloned.1.call-start = ((), (), s32[]{:S(2)}) async-start(), calls=%async_computation.1 | async-start | bytes 4456448 | tf_op jit(solution)/shard_map/all_gather | solution.py:88
  158.5 41.0 %collective-permute-start = (bf16[1,256,2048]{2,1,0:T(8,128)(2,1)S(1)}, bf16[1,256,2048]{2,1,0:T(8,128)(2,1)S(1)}, u32[]{:S(2)}, u32[]{:S(2)}) collective-permute-start(bf16[1,256,2048]{2,1,0:T(8,128)(2,1)S(1)} %slice_bitcast_fusion), channel_id=1, source_target_pairs={{0,16},{16,32},{32,48},{48,64},{64,80},{80,96},{96,112},{112,128},... | collective-permute-start | bytes 3145736 | tf_op jit(solution)/shard_map/ppermute | solution.py:14
  160.4 46.0 %collective-permute-start.1 = (bf16[1,256,2048]{2,1,0:T(8,128)(2,1)S(1)}, bf16[1,256,2048]{2,1,0:T(8,128)(2,1)S(1)}, u32[]{:S(2)}, u32[]{:S(2)}) collective-permute-start(bf16[1,256,2048]{2,1,0:T(8,128)(2,1)S(1)} %slice_bitcast_fusion), channel_id=1, source_target_pairs={{16,0},{32,16},{48,32},{64,48},{80,64},{96,80},{112,96},{128,112},... | collective-permute-start | bytes 3145736 | tf_op jit(solution)/shard_map/ppermute | solution.py:17
  170.1 57.9 %collective-permute-start.2 = (bf16[1,256,2048]{2,1,0:T(8,128)(2,1)S(1)}, bf16[1,256,2048]{2,1,0:T(8,128)(2,1)S(1)}, u32[]{:S(2)}, u32[]{:S(2)}) collective-permute-start(bf16[1,256,2048]{2,1,0:T(8,128)(2,1)S(1)} %slice_bitcast_fusion), channel_id=1, source_target_pairs={{0,1},{1,2},{2,3},{3,4},{4,5},{5,6},{6,7},{7,8},{8,9},{9,10},{10,1... | collective-permute-start | bytes 3145736 | tf_op jit(solution)/shard_map/ppermute | solution.py:14
  175.3 79.2 %collective-permute-start.3 = (bf16[1,256,2048]{2,1,0:T(8,128)(2,1)S(1)}, bf16[1,256,2048]{2,1,0:T(8,128)(2,1)S(1)}, u32[]{:S(2)}, u32[]{:S(2)}) collective-permute-start(bf16[1,256,2048]{2,1,0:T(8,128)(2,1)S(1)} %slice_bitcast_fusion), channel_id=1, source_target_pairs={{1,0},{2,1},{3,2},{4,3},{5,4},{6,5},{7,6},{8,7},{9,8},{10,9},{11,1... | collective-permute-start | bytes 3145736 | tf_op jit(solution)/shard_map/ppermute | solution.py:17
Sparse Core Ops, SparseCore 0:
  9.1 140.9 all-gather.2
  151.8 107.4 all-gather.4
where the time goes:
time: 285 us
  waiting for transfers between devices  216 us (76%)
  matrix products  29 us (10%)
  starting transfers between devices  18.9 us (7%)
  between operations  14.1 us (5%)
  other arithmetic  6.84 us (2%)
    all_gather x1, waiting for transfers between devices, per_device(): lax.all_gather(w_qkv, 'inner', axis=0, tiled=True)  140 us
    ppermute x2, waiting for transfers between devices, padded(): lax.ppermute(lax.slice_in_dim(block, block.shape[dim] - width, None, axis...  41.9 us
    ppermute x2, waiting for transfers between devices, padded(): lax.ppermute(lax.slice_in_dim(block, 0, width, axis=dim), axis, backward)  32.8 us
    ppermute x2, starting transfers between devices, padded(): lax.ppermute(lax.slice_in_dim(block, 0, width, axis=dim), axis, backward)  11.8 us
    dot_general x40, matrix products, per_device(): jnp.dot(rounded[:, slot_no * rows_here:(slot_no + 1) * rows_here], candid...  9.07 us
    dot_general x1, matrix products, per_device(): jnp.dot(normed, lax.all_gather(w_qkv, 'inner', axis=0, tiled=True), prefe...  8.16 us
    dot_general x40, matrix products, per_device(): jnp.einsum('qd,kd->qk', query_head, source_kv[:, offset_q:offset_q + head...  7.37 us
    ppermute x2, starting transfers between devices, padded(): lax.ppermute(lax.slice_in_dim(block, block.shape[dim] - width, None, axis...  7.12 us
  transfers between devices with their start and end apart: 6, of which 5 were waited for; matrix products, arithmetic and copies ran while one was open for 11% of the time, Pallas kernels for 0%

commit v1 on v0

--- a/solution.py
+++ b/solution.py
@@ -33,7 +33,9 @@
     head_size = HD
     projected = jnp.dot(
         normed,
-        lax.all_gather(w_qkv, "inner", axis=0, tiled=True),
+        jnp.concatenate(
+            lax.all_to_all(jnp.stack([w_qkv] * lax.axis_size("inner")), "inner", 0, 0), axis=0
+        ),
         preferred_element_type=jnp.float32,
     ).astype(jnp.bfloat16)
     queries = projected[:, :heads_all]

time: 285 us -> 436 us (1.53); the launches traced: 285 us -> 430 us
  waiting for transfers between devices: 216 us -> 322 us
  starting transfers between devices: 18.9 us -> 52.5 us
  local copies, waits for them, and re-layouts: 0.1 us -> 7.3 us
    all_to_all x0 -> x1, waiting for transfers between devices: none -> 293 us  [per_device(): lax.all_to_all(jnp.stack([w_qkv] * lax.axis_size('inner')), 'inner', 0, 0)]
    all_gather x1 -> x0, waiting for transfers between devices: 140 us -> none  [per_device(): lax.all_gather(w_qkv, 'inner', axis=0, tiled=True)]
    ppermute x2, waiting for transfers between devices: 41.9 us -> 11.1 us  [padded(): lax.ppermute(lax.slice_in_dim(block, block.shape[dim] - width, None, axis...]
    ppermute x2, starting transfers between devices: 7.12 us -> 34.5 us  [padded(): lax.ppermute(lax.slice_in_dim(block, block.shape[dim] - width, None, axis...]
    ppermute x2, waiting for transfers between devices: 32.8 us -> 17.1 us  [padded(): lax.ppermute(lax.slice_in_dim(block, 0, width, axis=dim), axis, backward)]
    another operation x0 -> x1, local copies, waits for them, and re-layouts: none -> 7.2 us  [per_device(): jnp.stack([w_qkv] * lax.axis_size('inner'))]
    all_to_all x0 -> x1, starting transfers between devices: none -> 6.2 us  [per_device(): lax.all_to_all(jnp.stack([w_qkv] * lax.axis_size('inner')), 'inner', 0, 0)]
  transfers between devices with their start and end apart: 6 -> 6, of which waited for: 5 -> 3; matrix products, arithmetic and copies ran while one was open for 11% -> 7% of each run, Pallas kernels for 0% -> 0%
where the time goes in v1:
time: 436 us; the launch traced here: 430 us
  waiting for transfers between devices  322 us (74%)
  starting transfers between devices  52.5 us (12%)
  matrix products  29 us (7%)
  between operations  14.1 us (3%)
  local copies, waits for them, and re-layouts  7.3 us (2%)
  other arithmetic  5.53 us (1%)
    all_to_all x1, waiting for transfers between devices, per_device(): lax.all_to_all(jnp.stack([w_qkv] * lax.axis_size('inner')), 'inner', 0, 0)  293 us
    ppermute x2, starting transfers between devices, padded(): lax.ppermute(lax.slice_in_dim(block, block.shape[dim] - width, None, axis...  34.5 us
    ppermute x2, waiting for transfers between devices, padded(): lax.ppermute(lax.slice_in_dim(block, 0, width, axis=dim), axis, backward)  17.1 us
    ppermute x2, starting transfers between devices, padded(): lax.ppermute(lax.slice_in_dim(block, 0, width, axis=dim), axis, backward)  11.8 us
    ppermute x2, waiting for transfers between devices, padded(): lax.ppermute(lax.slice_in_dim(block, block.shape[dim] - width, None, axis...  11.1 us
    dot_general x40, matrix products, per_device(): jnp.dot(rounded[:, slot_no * rows_here:(slot_no + 1) * rows_here], candid...  9.07 us
  transfers between devices with their start and end apart: 6, of which 3 were waited for; matrix products, arithmetic and copies ran while one was open for 7% of the time, Pallas kernels for 0%

profile of v1, /device:TPU:152, one launch (start us, length us, event | category | flops | bytes accessed | tf_op | source)
XLA Modules:
  0.0 430.2 jit_solution(13716540347844866143)
XLA Ops:
  6.5 7.2 %stack.2 = bf16[16,128,3072]{2,1,0:T(8,128)(2,1)} broadcast(bf16[128,3072]{1,0:T(8,128)(2,1)} %param.6), dimensions={1,2} | broadcast | bytes 13369344 | tf_op jit(solution)/shard_map/stack | solution.py:37
  13.7 6.2 %all-to-all-start = ((bf16[16,128,3072]{2,1,0:T(8,128)(2,1)}), bf16[16,128,3072]{2,1,0:T(8,128)(2,1)}, u32[]{:S(2)}, u32[]{:S(2)}) async-start(bf16[16,128,3072]{2,1,0:T(8,128)(2,1)} %stack.2), calls=%async_computation | async-start | bytes 25165824 | tf_op jit(solution)/shard_map/all_to_all | solution.py:37
  20.0 0.7 all-gather.2.cloned.1.call-update
  21.0 0.2 convert_reduce_fusion
  21.2 0.4 fusion.2
  21.7 292.9 %all-to-all-done = bf16[16,128,3072]{2,1,0:T(8,128)(2,1)} async-done(((bf16[16,128,3072]{2,1,0:T(8,128)(2,1)}), bf16[16,128,3072]{2,1,0:T(8,128)(2,1)}, u32[]{:S(2)}, u32[]{:S(2)}) %all-to-all-start) | async-done | bytes 12582944 | tf_op jit(solution)/shard_map/all_to_all | solution.py:37
  314.5 8.2 %convolution_convert_fusion = bf16[256,3072]{1,0:T(8,128)(2,1)S(1)} fusion(bf16[2048,3072]{1,0:T(8,128)(2,1)} %bitcast.2, bf16[256,2048]{1,0:T(8,128)(2,1)S(1)} %copy-done, f32[256]{0:T(256)S(1)} %add_rsqrt_fusion, f32[256]{0:T(256)S(1)} %broadcast_multiply_fusion), kind=kOutput, calls=%fused_computation | convolution fusion | flops 3224109056 | bytes 15206400 | tf_op jit(solution)/shard_map/dot_general | solution.py:34
  323.0 1.9 collective-permute-start
  324.9 9.7 %collective-permute-start.1 = (bf16[1,256,2048]{2,1,0:T(8,128)(2,1)S(1)}, bf16[1,256,2048]{2,1,0:T(8,128)(2,1)S(1)}, u32[]{:S(2)}, u32[]{:S(2)}) collective-permute-start(bf16[1,256,2048]{2,1,0:T(8,128)(2,1)S(1)} %slice_bitcast_fusion), channel_id=1, source_target_pairs={{16,0},{32,16},{48,32},{64,48},{80,64},{96,80},{112,96},{128,112},... | collective-permute-start | bytes 3145736 | tf_op jit(solution)/shard_map/ppermute | solution.py:17
  334.6 32.6 %collective-permute-start.2 = (bf16[1,256,2048]{2,1,0:T(8,128)(2,1)S(1)}, bf16[1,256,2048]{2,1,0:T(8,128)(2,1)S(1)}, u32[]{:S(2)}, u32[]{:S(2)}) collective-permute-start(bf16[1,256,2048]{2,1,0:T(8,128)(2,1)S(1)} %slice_bitcast_fusion), channel_id=1, source_target_pairs={{0,1},{1,2},{2,3},{3,4},{4,5},{5,6},{6,7},{7,8},{8,9},{9,10},{10,1... | collective-permute-start | bytes 3145736 | tf_op jit(solution)/shard_map/ppermute | solution.py:14
  367.2 2.1 collective-permute-start.3
  369.5 0.2 convolution_dynamic-update-slice_fusion.34
  370.0 0.2 convolution_dynamic-update-slice_fusion.19
  370.2 0.2 convolution_dynamic-update-slice_fusion.14
  370.4 0.2 convolution_dynamic-update-slice_fusion.9
  370.8 0.2 convolution_dynamic-update-slice_fusion.38
  371.2 0.2 convolution_dynamic-update-slice_fusion.37
  371.4 11.1 %collective-permute-done.2 = bf16[1,256,2048]{2,1,0:T(8,128)(2,1)S(1)} collective-permute-done((bf16[1,256,2048]{2,1,0:T(8,128)(2,1)S(1)}, bf16[1,256,2048]{2,1,0:T(8,128)(2,1)S(1)}, u32[]{:S(2)}, u32[]{:S(2)}) %collective-permute-start.2) | collective-permute-done | bytes 1048608 | tf_op jit(solution)/shard_map/ppermute | solution.py:14
  382.9 17.1 %collective-permute-done.3 = bf16[1,256,2048]{2,1,0:T(8,128)(2,1)S(1)} collective-permute-done((bf16[1,256,2048]{2,1,0:T(8,128)(2,1)S(1)}, bf16[1,256,2048]{2,1,0:T(8,128)(2,1)S(1)}, u32[]{:S(2)}, u32[]{:S(2)}) %collective-permute-start.3) | collective-permute-done | bytes 1048608 | tf_op jit(solution)/shard_map/ppermute | solution.py:17
  400.1 0.2 convolution_dynamic-update-slice_fusion.35
  404.9 0.4 fusion.11
  405.3 2.0 fusion.69
  407.3 0.2 fusion.127
  407.5 0.2 fusion.129
  407.7 0.2 fusion.133
  408.0 2.3 fusion.67
  410.3 0.2 fusion.119
  410.5 0.2 fusion.121
  410.7 0.2 fusion.125
  410.9 0.2 fusion.111
  411.2 0.2 fusion.113
  411.4 0.2 fusion.117
  411.6 0.2 fusion.103
  411.9 0.2 fusion.105
  412.1 0.2 fusion.109
  412.3 0.2 fusion.95
  412.6 0.2 fusion.97
  412.8 0.2 fusion.101
  413.0 0.2 fusion.87
  413.2 0.2 fusion.89
  413.5 0.2 fusion.93
  413.7 0.2 fusion.79
  413.9 0.2 fusion.81
  414.2 0.2 fusion.85
  414.4 0.2 fusion.71
  414.6 0.2 fusion.73
  414.8 0.2 fusion.77
  415.1 0.2 convolution_add_fusion.15
  415.3 0.2 convolution_add_fusion.13
  415.5 0.2 convolution_add_fusion.11
  415.8 0.2 convolution_add_fusion.9
  416.0 0.2 convolution_add_fusion.7
  416.2 0.2 convolution_add_fusion.5
  416.5 0.2 convolution_add_fusion.3
  416.7 0.2 convolution_add_fusion.1
  416.9 0.2 fusion.51
  417.2 0.2 fusion.49
  417.4 0.2 fusion.47
  417.7 0.2 fusion.45
  417.9 0.2 fusion.43
  418.2 0.2 fusion.41
  418.4 0.2 fusion.39
  418.7 0.2 fusion.37
  419.0 4.4 %convolution_convert_fusion.1 = bf16[256,2048]{1,0:T(8,128)(2,1)} fusion(bf16[256,1024]{1,0:T(8,128)(2,1)S(1)} %fusion.37, bf16[1024,2048]{1,0:T(8,128)(2,1)} %all-gather.2.cloned.1.call-done), kind=kOutput, calls=%fused_computation.3 | convolution fusion | flops 1074266112 | bytes 5767168 | tf_op jit(solution)/shard_map/dot_general | solution.py:88
  (51 shorter events, 6.5 us)
Async XLA Ops:
  13.7 6.9 %copy-start.2 = (s32[1,5]{1,0:T(1,128)S(1)}, s32[1,5]{1,0:T(1,128)}, u32[]{:S(2)}) copy-start(s32[1,5]{1,0:T(1,128)} %param.8) | copy-start | bytes 64
  13.7 7.0 %copy-start.1 = (s32[256]{0:T(256)S(1)}, s32[256]{0:T(256)}, u32[]{:S(2)}) copy-start(s32[256]{0:T(256)} %param.9) | copy-start | bytes 3076
  13.7 7.3 %copy-start = (bf16[256,2048]{1,0:T(8,128)(2,1)S(1)}, bf16[256,2048]{1,0:T(8,128)(2,1)}, u32[]{:S(2)}) copy-start(bf16[256,2048]{1,0:T(8,128)(2,1)} %param.5) | copy-start | bytes 3145732
  13.7 300.8 %all-to-all-start = ((bf16[16,128,3072]{2,1,0:T(8,128)(2,1)}), bf16[16,128,3072]{2,1,0:T(8,128)(2,1)}, u32[]{:S(2)}, u32[]{:S(2)}) async-start(bf16[16,128,3072]{2,1,0:T(8,128)(2,1)} %stack.2), calls=%async_computation | async-start | bytes 25165824 | tf_op jit(solution)/shard_map/all_to_all | solution.py:37
  19.9 399.0 %all-gather.2.cloned.1.call-start = ((), (), s32[]{:S(2)}) async-start(), calls=%async_computation.1 | async-start | bytes 4456448 | tf_op jit(solution)/shard_map/all_gather | solution.py:90
  323.0 47.7 %collective-permute-start = (bf16[1,256,2048]{2,1,0:T(8,128)(2,1)S(1)}, bf16[1,256,2048]{2,1,0:T(8,128)(2,1)S(1)}, u32[]{:S(2)}, u32[]{:S(2)}) collective-permute-start(bf16[1,256,2048]{2,1,0:T(8,128)(2,1)S(1)} %slice_bitcast_fusion), channel_id=1, source_target_pairs={{0,16},{16,32},{32,48},{48,64},{64,80},{80,96},{96,112},{112,128},... | collective-permute-start | bytes 3145736 | tf_op jit(solution)/shard_map/ppermute | solution.py:14
  324.9 46.1 %collective-permute-start.1 = (bf16[1,256,2048]{2,1,0:T(8,128)(2,1)S(1)}, bf16[1,256,2048]{2,1,0:T(8,128)(2,1)S(1)}, u32[]{:S(2)}, u32[]{:S(2)}) collective-permute-start(bf16[1,256,2048]{2,1,0:T(8,128)(2,1)S(1)} %slice_bitcast_fusion), channel_id=1, source_target_pairs={{16,0},{32,16},{48,32},{64,48},{80,64},{96,80},{112,96},{128,112},... | collective-permute-start | bytes 3145736 | tf_op jit(solution)/shard_map/ppermute | solution.py:17
  334.6 47.9 %collective-permute-start.2 = (bf16[1,256,2048]{2,1,0:T(8,128)(2,1)S(1)}, bf16[1,256,2048]{2,1,0:T(8,128)(2,1)S(1)}, u32[]{:S(2)}, u32[]{:S(2)}) collective-permute-start(bf16[1,256,2048]{2,1,0:T(8,128)(2,1)S(1)} %slice_bitcast_fusion), channel_id=1, source_target_pairs={{0,1},{1,2},{2,3},{3,4},{4,5},{5,6},{6,7},{7,8},{8,9},{9,10},{10,1... | collective-permute-start | bytes 3145736 | tf_op jit(solution)/shard_map/ppermute | solution.py:14
  367.2 32.8 %collective-permute-start.3 = (bf16[1,256,2048]{2,1,0:T(8,128)(2,1)S(1)}, bf16[1,256,2048]{2,1,0:T(8,128)(2,1)S(1)}, u32[]{:S(2)}, u32[]{:S(2)}) collective-permute-start(bf16[1,256,2048]{2,1,0:T(8,128)(2,1)S(1)} %slice_bitcast_fusion), channel_id=1, source_target_pairs={{1,0},{2,1},{3,2},{4,3},{5,4},{6,5},{7,6},{8,7},{9,8},{10,9},{11,1... | collective-permute-start | bytes 3145736 | tf_op jit(solution)/shard_map/ppermute | solution.py:17
Sparse Core Ops, SparseCore 0:
  22.5 294.2 all-gather.1
